TPU v7x, 128 devices: a whole 4x4x4 slice. The times are simulated.
128 devices in a mesh: req: 32 (over y, z, core), grp: 4 (over x).
Axes of the slice: x: 4, y: 4, z: 4, core: 2. Of those that a mesh axis runs over, the one named last changes fastest.
Arguments:
- hidden_in: bfloat16 [16384, 2048], P('req'), may hold values from -6 to 6
- attn_gain: float32 [2048], replicated, may hold values from 0.1 to 1.9
- mlp_gain: float32 [2048], replicated, may hold values from 0.1 to 1.9
- w_query: bfloat16 [2048, 2048], P(None, 'grp'), may hold values from -0.75 to 0.75
- w_key: bfloat16 [2048, 512], P(None, 'grp'), may hold values from -0.125 to 0.125
- w_value: bfloat16 [2048, 512], P(None, 'grp'), may hold values from -0.125 to 0.125
- w_out: bfloat16 [2048, 2048], P('grp'), may hold values from -0.125 to 0.125
- w_gate: bfloat16 [2048, 8192], P(None, 'req'), may hold values from -0.125 to 0.125
- w_up: bfloat16 [2048, 8192], P(None, 'req'), may hold values from -0.125 to 0.125
- w_down: bfloat16 [8192, 2048], P('req'), may hold values from -0.0625 to 0.0625
- cache_k: bfloat16 [16384, 16, 512], P('req', None, 'grp'), may hold values from -4000 to 4000
- cache_v: bfloat16 [16384, 16, 512], P('req', None, 'grp'), may hold values from -6 to 6
- owner_of_row: int32 [16384], P('req'), may hold values from 0 to 31, as said below
- new_len: int32 [32, 32], P('req'), may hold values from 0 to 32, as said below
- prior_len: int32 [32, 32], P('req'), may hold values from 0 to 256, as said below
- page_table: int32 [32, 512], P('req'), may hold values from 0 to 511, each once within a row
Outputs:
- layer_out: bfloat16 [16384, 2048], P(('req', 'grp'))
- new_cache_k: bfloat16 [16384, 16, 512], P('req', None, 'grp')
- new_cache_v: bfloat16 [16384, 16, 512], P('req', None, 'grp')
Inputs may be any that keep to these rules, and one draw needn't show every extreme that they name: `owner_of_row`: rows of one block of 512 that name the same owner are consecutive; each block holds at most one request for each owner, of at most 32 rows; in every draw one owner receives a request of exactly 32 rows from every block. new_len[o, s] is the number of rows of block s of owner_of_row that name o. prior_len[o, s] + new_len[o, s] <= 256.
All inputs are finite; a program needn't handle non-finite values.
Results may differ from a plain program's by a relative error of at most 0.0063.
Values may be sent and summed in bfloat16 or wider, within the bound.
A program may use at most 128 MiB of HBM per device.

v0:
```python
import jax
import jax.numpy as jnp
from jax import lax
from jax.sharding import PartitionSpec as P

HD = 64
PAGE = 16
MAXP = 16
CONTEXT = 256
EPSILON = 1e-05
RESIDUAL_MULT = 0.22
SCORE_MULT = 0.015625
ROPE_BASE = 10000000.0


def normalize(values, gain):
    mean_square = jnp.mean(values * values, axis=-1, keepdims=True)
    return values * lax.rsqrt(mean_square + EPSILON) * gain


def rotary(values, positions):
    dim = values.shape[-1]
    half = dim // 2
    freq = jnp.power(ROPE_BASE, -2.0 * jnp.arange(half, dtype=jnp.int32).astype(jnp.float32) / dim)
    angle = positions.astype(jnp.float32)[:, :, None] * freq
    cosine = jnp.cos(angle)[:, :, None, :]
    sine = jnp.sin(angle)[:, :, None, :]
    first = values[..., :half].astype(jnp.float32)
    second = values[..., half:].astype(jnp.float32)
    return jnp.concatenate(
        [first * cosine - second * sine, second * cosine + first * sine], axis=-1
    )


def source_layout(owner_block, peers, pair_rows):
    row_count = owner_block.shape[0]
    owners = jnp.arange(peers, dtype=jnp.int32)
    member = owner_block[None, :] == owners[:, None]
    counts = jnp.sum(member.astype(jnp.int32), axis=1)
    row_ids = jnp.arange(row_count, dtype=jnp.int32)
    starts = jnp.min(jnp.where(member, row_ids[None, :], row_count), axis=1)
    slots = jnp.arange(pair_rows, dtype=jnp.int32)
    gather_rows = jnp.where(
        slots[None, :] < counts[:, None], starts[:, None] + slots[None, :], row_count
    )
    row_start = jnp.sum(jnp.where(member, starts[:, None], 0), axis=0)
    back_rows = owner_block * pair_rows + (row_ids - row_start)
    return (gather_rows.reshape(-1), back_rows)


def owner_attention(query_in, key_in, value_in, cache_keys, cache_values, lengths, priors, table):
    sources, pair_rows, qcols = query_in.shape
    kcols = key_in.shape[-1]
    kv_heads = kcols // HD
    group = qcols // kcols
    pool_pages = cache_keys.shape[0]
    slots = jnp.arange(pair_rows, dtype=jnp.int32)
    positions = priors[:, None] + slots[None, :]
    live = slots[None, :] < lengths[:, None]
    query_rot = rotary(query_in.reshape(sources, pair_rows, qcols // HD, HD), positions).astype(
        jnp.bfloat16
    )
    key_rot = rotary(key_in.reshape(sources, pair_rows, kv_heads, HD), positions).astype(
        jnp.bfloat16
    )
    key_rot = key_rot.reshape(sources, pair_rows, kcols)
    pages = table.reshape(sources, MAXP)
    page_index = jnp.minimum(positions // PAGE, MAXP - 1)
    target = jnp.take_along_axis(pages, page_index, axis=1)
    target = jnp.where(live, target, pool_pages).reshape(-1)
    offset = (positions % PAGE).reshape(-1)
    keys_out = cache_keys.at[target, offset].set(key_rot.reshape(-1, kcols), mode="drop")
    values_out = cache_values.at[target, offset].set(value_in.reshape(-1, kcols), mode="drop")
    key_block = jnp.take(keys_out, pages.reshape(-1), axis=0).reshape(
        sources, CONTEXT, kv_heads, HD
    )
    value_block = jnp.take(values_out, pages.reshape(-1), axis=0).reshape(
        sources, CONTEXT, kv_heads, HD
    )
    grouped = query_rot.reshape(sources, pair_rows, kv_heads, group, HD)
    scores = (
        jnp.einsum("stkgd,sjkd->skgtj", grouped, key_block, preferred_element_type=jnp.float32)
        * SCORE_MULT
    )
    allowed = (
        jnp.arange(CONTEXT, dtype=jnp.int32)[None, None, None, None, :]
        <= positions[:, None, None, :, None]
    )
    scores = jnp.where(allowed, scores, -jnp.inf)
    top = jnp.max(scores, axis=-1, keepdims=True)
    weights = jnp.exp(scores - top)
    probs = (weights / jnp.sum(weights, axis=-1, keepdims=True)).astype(jnp.bfloat16)
    mixed = jnp.einsum("skgtj,sjkd->stkgd", probs, value_block, preferred_element_type=jnp.float32)
    return (mixed.astype(jnp.bfloat16).reshape(sources, pair_rows, qcols), keys_out, values_out)


def body(
    hidden_in,
    attn_gain,
    mlp_gain,
    w_query,
    w_key,
    w_value,
    w_out,
    w_gate,
    w_up,
    w_down,
    cache_k,
    cache_v,
    owner_of_row,
    new_len,
    prior_len,
    page_table,
):
    peers = lax.axis_size("req")
    groups = lax.axis_size("grp")
    row_count = hidden_in.shape[0]
    pair_rows = 2 * row_count // peers
    quarter = row_count // groups
    group_index = lax.axis_index("grp")
    normed = normalize(hidden_in.astype(jnp.float32), attn_gain).astype(jnp.bfloat16)
    query_rows = jnp.dot(normed, w_query, preferred_element_type=jnp.float32).astype(jnp.bfloat16)
    key_rows = jnp.dot(normed, w_key, preferred_element_type=jnp.float32).astype(jnp.bfloat16)
    value_rows = jnp.dot(normed, w_value, preferred_element_type=jnp.float32).astype(jnp.bfloat16)
    gather_rows, back_rows = source_layout(owner_of_row, peers, pair_rows)
    send_query = jnp.take(query_rows, gather_rows, axis=0, mode="fill", fill_value=0).reshape(
        peers, pair_rows, -1
    )
    send_key = jnp.take(key_rows, gather_rows, axis=0, mode="fill", fill_value=0).reshape(
        peers, pair_rows, -1
    )
    send_value = jnp.take(value_rows, gather_rows, axis=0, mode="fill", fill_value=0).reshape(
        peers, pair_rows, -1
    )
    recv_query, recv_key, recv_value = (
        lax.all_to_all(send_query, "req", split_axis=0, concat_axis=0, tiled=True),
        lax.all_to_all(send_key, "req", split_axis=0, concat_axis=0, tiled=True),
        lax.all_to_all(send_value, "req", split_axis=0, concat_axis=0, tiled=True),
    )
    mixed, keys_out, values_out = owner_attention(
        recv_query, recv_key, recv_value, cache_k, cache_v, new_len[0], prior_len[0], page_table[0]
    )
    returned = lax.all_to_all(mixed, "req", split_axis=0, concat_axis=0, tiled=True)
    attn_rows = jnp.take(returned.reshape(peers * pair_rows, -1), back_rows, axis=0)
    projected = jnp.dot(attn_rows, w_out, preferred_element_type=jnp.float32)
    total = lax.psum(projected.astype(jnp.bfloat16), "grp").astype(jnp.float32)
    attn_part = lax.dynamic_slice_in_dim(total, group_index * quarter, quarter, 0)
    own_rows = lax.dynamic_slice_in_dim(hidden_in, group_index * quarter, quarter, 0).astype(
        jnp.float32
    )
    residual = own_rows + RESIDUAL_MULT * attn_part
    mlp_in = normalize(residual, mlp_gain).astype(jnp.bfloat16)
    piece = lax.all_gather(mlp_in, "req", axis=0, tiled=True)
    gate = jnp.dot(piece, w_gate, preferred_element_type=jnp.float32)
    upper = jnp.dot(piece, w_up, preferred_element_type=jnp.float32)
    hidden = (jax.nn.silu(gate) * upper).astype(jnp.bfloat16)
    down = lax.psum_scatter(
        jnp.dot(hidden, w_down, preferred_element_type=jnp.float32).astype(jnp.bfloat16),
        "req",
        scatter_dimension=0,
        tiled=True,
    ).astype(jnp.float32)
    layer_out = (residual + RESIDUAL_MULT * down).astype(jnp.bfloat16)
    return (layer_out, keys_out, values_out)


def solution(mesh):
    in_specs = (
        P("req", None),
        P(),
        P(),
        P(None, "grp"),
        P(None, "grp"),
        P(None, "grp"),
        P("grp", None),
        P(None, "req"),
        P(None, "req"),
        P("req", None),
        P("req", None, "grp"),
        P("req", None, "grp"),
        P("req"),
        P("req", None),
        P("req", None),
        P("req", None),
    )
    out_specs = (P(("req", "grp"), None), P("req", None, "grp"), P("req", None, "grp"))
    return jax.shard_map(body, mesh=mesh, in_specs=in_specs, out_specs=out_specs, check_vma=False)
```

profile of v0, /device:TPU:0, one launch (start us, length us, event | category | flops | bytes accessed | tf_op | source)
XLA Modules:
  0.0 475.2 jit_solution(9839665422419617770)
XLA Ops:
  26.3 8.4 %all-to-all-start.1 = ((bf16[32,32,128]{2,1,0:T(8,128)(2,1)}), bf16[32,32,128]{2,1,0:T(8,128)(2,1)S(1)}, u32[]{:S(2)}, u32[]{:S(2)}) async-start(bf16[32,32,128]{2,1,0:T(8,128)(2,1)} %bitcast.10), calls=%async_computation.1 | async-start | bytes 524288 | tf_op jit(solution)/shard_map/all_to_all | solution.py:137
  37.1 7.1 %gather_fusion.2 = s32[1024]{0:T(1024)S(1)} fusion(s32[32,16]{1,0:T(8,128)S(1)} %reshape_squeeze.3, s32[1024]{0:T(1024)S(1)} %reshape.573), kind=kCustom, calls=%fused_computation.6 | custom fusion | bytes 16384 | tf_op jit(solution)/shard_map/jit(take_along_axis)/gather | solution.py:69
  48.0 5.1 %gather_fusion = bf16[1024,512]{1,0:T(8,128)(2,1)} fusion(bf16[512,512]{1,0:T(8,128)(2,1)S(1)} %convolution_convert_fusion.2, s32[1024]{0:T(1024)S(1)} %broadcast_clamp_fusion), kind=kCustom, calls=%fused_computation.4 | custom fusion | bytes 2101248 | tf_op jit(solution)/shard_map/jit(_take)/gather | solution.py:126
  56.4 7.5 %all-to-all-start = ((bf16[32,32,128]{2,1,0:T(8,128)(2,1)}), bf16[32,32,128]{2,1,0:T(8,128)(2,1)}, u32[]{:S(2)}, u32[]{:S(2)}) async-start(bf16[32,32,128]{2,1,0:T(8,128)(2,1)} %bitcast.5), calls=%async_computation | async-start | bytes 524288 | tf_op jit(solution)/shard_map/all_to_all | solution.py:138
  67.1 5.7 %all-to-all-done = bf16[32,32,128]{2,1,0:T(8,128)(2,1)} async-done(((bf16[32,32,128]{2,1,0:T(8,128)(2,1)}), bf16[32,32,128]{2,1,0:T(8,128)(2,1)}, u32[]{:S(2)}, u32[]{:S(2)}) %all-to-all-start) | async-done | bytes 262176 | tf_op jit(solution)/shard_map/all_to_all | solution.py:138
  72.9 5.1 %all-to-all-start.2 = ((bf16[32,32,512]{2,1,0:T(8,128)(2,1)}), bf16[32,32,512]{2,1,0:T(8,128)(2,1)}, u32[]{:S(2)}, u32[]{:S(2)}) async-start(bf16[32,32,512]{2,1,0:T(8,128)(2,1)} %broadcast_select_fusion.2), calls=%async_computation.2 | async-start | bytes 2097152 | tf_op jit(solution)/shard_map/all_to_all | solution.py:136
  81.6 6.5 %scatter_fusion.1 = bf16[8192,128]{1,0:T(8,128)(2,1)} fusion(bf16[8192,128]{1,0:T(8,128)(2,1)} %bitcast.52, s32[1024]{0:T(1024)S(1)} %broadcast_select_fusion.5, bf16[1024,128]{1,0:T(8,128)(2,1)S(1)} %reshape.587), kind=kCustom, calls=%fused_computation.8 | custom fusion | bytes 790528
  88.0 4.0 gather_fusion.6
  92.0 6.9 %scatter_fusion = bf16[8192,128]{1,0:T(8,128)(2,1)} fusion(bf16[8192,128]{1,0:T(8,128)(2,1)} %bitcast.49, s32[1024]{0:T(1024)S(1)} %broadcast_select_fusion.5, bf16[1024,128]{1,0:T(8,128)(2,1)} %bitcast.6), kind=kCustom, calls=%fused_computation.7 | custom fusion | bytes 790528
  98.9 4.0 gather_fusion.4
  102.9 4.6 broadcast_select_fusion.1
  107.5 8.2 %reshape.510 = bf16[32,256,2,64]{3,2,1,0:T(2,128)(2,1)} reshape(bf16[512,16,128]{2,1,0:T(8,128)(2,1)} %get-tuple-element.22) | data formatting | bytes 4194304 | tf_op jit(solution)/shard_map/reshape | solution.py:77
  115.7 8.3 %reshape.513 = bf16[32,256,2,64]{3,2,1,0:T(2,128)(2,1)} reshape(bf16[512,16,128]{2,1,0:T(8,128)(2,1)} %get-tuple-element.23) | data formatting | bytes 4194304 | tf_op jit(solution)/shard_map/reshape | solution.py:74
  127.9 4.0 fusion.7
  135.8 4.9 %fusion.49 = (f32[32,2,4,32]{3,2,1,0:T(4,128)S(1)}, f32[32,2,4,32,256]{4,3,2,1,0:T(8,128)}) fusion(f32[32,2,256,32,4]{2,3,4,1,0:T(8,128)S(1)} %fusion.10, pred[32,32,256]{2,1,0:T(8,128)(4,1)S(1)} %copy-done.6), kind=kOutput, calls=%fused_computation.132 | output fusion | flops 12583167 | bytes 17072128 | tf_op jit(solution)/shard_map/sub | solution.py:91
  140.7 4.5 convert_bitcast_fusion
  147.7 4.7 reshape.515
  152.4 7.5 %all-to-all-start.3 = ((bf16[32,32,512]{2,1,0:T(8,128)(2,1)}), bf16[32,32,512]{2,1,0:T(8,128)(2,1)S(1)}, u32[]{:S(2)}, u32[]{:S(2)}) async-start(bf16[32,32,512]{2,1,0:T(8,128)(2,1)} %reshape.515), calls=%async_computation.3 | async-start | bytes 2097152 | tf_op jit(solution)/shard_map/all_to_all | solution.py:143
  159.9 16.7 %all-to-all-done.3 = bf16[32,32,512]{2,1,0:T(8,128)(2,1)S(1)} async-done(((bf16[32,32,512]{2,1,0:T(8,128)(2,1)}), bf16[32,32,512]{2,1,0:T(8,128)(2,1)S(1)}, u32[]{:S(2)}, u32[]{:S(2)}) %all-to-all-start.3) | async-done | bytes 1048608 | tf_op jit(solution)/shard_map/all_to_all | solution.py:143
  183.1 56.8 %all-reduce.2.cloned.1.call-done = bf16[512,2048]{1,0:T(8,128)(2,1)} async-done(((bf16[512,2048]{1,0:T(8,128)(2,1)}), bf16[512,2048]{1,0:T(8,128)(2,1)}) %all-reduce.2.cloned.1.call-update) | async-done | bytes 2097168 | tf_op jit(solution)/shard_map/psum | solution.py:146
  243.7 72.5 %all-gather.2.cloned.1.call-done = bf16[4096,2048]{1,0:T(8,128)(2,1)} async-done(((bf16[128,2048]{1,0:T(8,128)(2,1)}), bf16[4096,2048]{1,0:T(8,128)(2,1)}) %all-gather.2.cloned.1.call-update) | async-done | bytes 16777232 | tf_op jit(solution)/shard_map/all_gather | solution.py:153
  316.2 10.2 %fusion.50 = f32[4096,256]{1,0:T(8,128)} fusion(bf16[4096,2048]{1,0:T(8,128)(2,1)} %all-gather.2.cloned.1.call-done, bf16[2048,256]{1,0:T(8,128)(2,1)S(1)} %copy-done.14), kind=kOutput, calls=%fused_computation.133 | convolution fusion | flops 4294967296 | bytes 22020096 | tf_op jit(solution)/shard_map/dot_general | solution.py:154
  326.4 24.7 %convolution_convert_fusion = bf16[4096,2048]{1,0:T(8,128)(2,1)} fusion(bf16[256,2048]{1,0:T(8,128)(2,1)} %param.29, bf16[4096,2048]{1,0:T(8,128)(2,1)} %all-gather.2.cloned.1.call-done, bf16[2048,256]{1,0:T(8,128)(2,1)} %param.28, f32[4096,256]{1,0:T(8,128)} %fusion.50), kind=kOutput, calls=%fused_computation.10 | convolution fusion | flops 8604614656 | bytes 39845888 | tf_op jit(solution)/shard_map/dot_general | solution.py:158
  351.2 114.9 %reduce-scatter.2.cloned.1.call-done = bf16[128,2048]{1,0:T(8,128)(2,1)} async-done(((bf16[4096,2048]{1,0:T(8,128)(2,1)}), bf16[128,2048]{1,0:T(8,128)(2,1)}) %reduce-scatter.2.cloned.1.call-update) | async-done | bytes 524304 | tf_op jit(solution)/shard_map/reduce_scatter | solution.py:157
  (108 shorter events, 58.0 us)
Async XLA Ops:
  7.2 172.1 %copy-start = (bf16[512,2048]{1,0:T(8,128)(2,1)S(1)}, bf16[512,2048]{1,0:T(8,128)(2,1)}, u32[]{:S(2)}) copy-start(bf16[512,2048]{1,0:T(8,128)(2,1)} %param.26) | copy-start | bytes 6291460
  7.2 3.4 copy-start.5
  7.2 4.8 %copy-start.8 = (s32[512]{0:T(512)S(1)}, s32[512]{0:T(512)}, u32[]{:S(2)}) copy-start(s32[512]{0:T(512)} %param.32) | copy-start | bytes 6148
  10.6 4.0 copy-start.15
  10.6 4.0 copy-start.16
  12.3 4.6 copy-start.2
  18.8 15.9 %copy-start.7 = (s32[1,512]{1,0:T(1,128)S(1)}, s32[1,512]{1,0:T(1,128)}, u32[]{:S(2)}) copy-start(s32[1,512]{1,0:T(1,128)} %param.35) | copy-start | bytes 6148
  18.8 16.0 %copy-start.10 = (s32[1,32]{1,0:T(1,128)S(1)}, s32[1,32]{1,0:T(1,128)}, u32[]{:S(2)}) copy-start(s32[1,32]{1,0:T(1,128)} %param.34) | copy-start | bytes 388
  18.8 17.6 %copy-start.11 = (s32[1,32]{1,0:T(1,128)S(1)}, s32[1,32]{1,0:T(1,128)}, u32[]{:S(2)}) copy-start(s32[1,32]{1,0:T(1,128)} %param.33) | copy-start | bytes 388
  26.3 30.1 %all-to-all-start.1 = ((bf16[32,32,128]{2,1,0:T(8,128)(2,1)}), bf16[32,32,128]{2,1,0:T(8,128)(2,1)S(1)}, u32[]{:S(2)}, u32[]{:S(2)}) async-start(bf16[32,32,128]{2,1,0:T(8,128)(2,1)} %bitcast.10), calls=%async_computation.1 | async-start | bytes 524288 | tf_op jit(solution)/shard_map/all_to_all | solution.py:137
  37.1 7.2 %copy-start.13 = (s32[2]{0:T(128)S(1)}, s32[2]{0:T(128)}, u32[]{:S(2)}) copy-start(s32[2]{0:T(128)} %constant.139) | copy-start | bytes 28
  37.1 7.3 %copy-start.12 = (s32[2]{0:T(128)S(1)}, s32[2]{0:T(128)}, u32[]{:S(2)}) copy-start(s32[2]{0:T(128)} %constant.136) | copy-start | bytes 28
  56.4 16.4 %all-to-all-start = ((bf16[32,32,128]{2,1,0:T(8,128)(2,1)}), bf16[32,32,128]{2,1,0:T(8,128)(2,1)}, u32[]{:S(2)}, u32[]{:S(2)}) async-start(bf16[32,32,128]{2,1,0:T(8,128)(2,1)} %bitcast.5), calls=%async_computation | async-start | bytes 524288 | tf_op jit(solution)/shard_map/all_to_all | solution.py:138
  72.9 51.2 %all-to-all-start.2 = ((bf16[32,32,512]{2,1,0:T(8,128)(2,1)}), bf16[32,32,512]{2,1,0:T(8,128)(2,1)}, u32[]{:S(2)}, u32[]{:S(2)}) async-start(bf16[32,32,512]{2,1,0:T(8,128)(2,1)} %broadcast_select_fusion.2), calls=%async_computation.2 | async-start | bytes 2097152 | tf_op jit(solution)/shard_map/all_to_all | solution.py:136
  115.7 12.2 %copy-start.3 = (f32[32,32,32]{2,1,0:T(8,128)S(1)}, f32[32,32,32]{2,1,0:T(8,128)}, u32[]{:S(2)}) copy-start(f32[32,32,32]{2,1,0:T(8,128)} %get-tuple-element.16) | copy-start | bytes 393220
  131.9 2.2 copy-start.1
  134.1 1.7 copy-start.6
  135.8 4.9 %copy-start.4 = (bf16[32,256,2,64]{3,2,1,0:T(2,128)(2,1)S(1)}, bf16[32,256,2,64]{3,2,1,0:T(2,128)(2,1)}, u32[]{:S(2)}) copy-start(bf16[32,256,2,64]{3,2,1,0:T(2,128)(2,1)} %reshape.510) | copy-start | bytes 6291460
  152.4 24.3 %all-to-all-start.3 = ((bf16[32,32,512]{2,1,0:T(8,128)(2,1)}), bf16[32,32,512]{2,1,0:T(8,128)(2,1)S(1)}, u32[]{:S(2)}, u32[]{:S(2)}) async-start(bf16[32,32,512]{2,1,0:T(8,128)(2,1)} %reshape.515), calls=%async_computation.3 | async-start | bytes 2097152 | tf_op jit(solution)/shard_map/all_to_all | solution.py:143
  159.8 80.0 %all-reduce.2.cloned.1.call-start = ((), (), s32[]{:S(2)}) async-start(), calls=%async_computation.5 | async-start | bytes 4194304 | tf_op jit(solution)/shard_map/psum | solution.py:146
  179.3 62.1 %copy-start.9 = (f32[2048]{0:T(1024)S(1)}, f32[2048]{0:T(1024)}, u32[]{:S(2)}) copy-start(f32[2048]{0:T(1024)} %param.22) | copy-start | bytes 24580
  183.0 133.2 %copy-start.14 = (bf16[2048,256]{1,0:T(8,128)(2,1)S(1)}, bf16[2048,256]{1,0:T(8,128)(2,1)}, u32[]{:S(2)}) copy-start(bf16[2048,256]{1,0:T(8,128)(2,1)} %param.27) | copy-start | bytes 3145732
  183.0 133.2 %all-gather.2.cloned.1.call-start = ((), (), s32[]{:S(2)}) async-start(), calls=%async_computation.6 | async-start | bytes 17301504 | tf_op jit(solution)/shard_map/all_gather | solution.py:153
  243.6 222.4 %reduce-scatter.2.cloned.1.call-start = ((), (), s32[]{:S(2)}) async-start(), calls=%async_computation.7 | async-start | bytes 17301504 | tf_op jit(solution)/shard_map/reduce_scatter | solution.py:157
Sparse Core Ops, SparseCore 0:
  183.1 56.6 all-reduce.1
  243.8 72.4 all-gather.1
  351.3 114.7 reduce-scatter.1
where the time goes:
time: 482 us; the launch traced here: 475 us
  waiting for transfers between devices  267 us (55%)
  local copies, waits for them, and re-layouts  80.5 us (17%)
  matrix products  52.5 us (11%)
  other arithmetic  32.4 us (7%)
  starting transfers between devices  28.7 us (6%)
  between operations  14.4 us (3%)
    reduce_scatter x1, waiting for transfers between devices, body(): lax.psum_scatter(jnp.dot(hidden, w_down, preferred_element_type=jnp.float...  115 us
    all_gather x1, waiting for transfers between devices, body(): piece = lax.all_gather(mlp_in, 'req', axis=0, tiled=True)  72.5 us
    psum x1, waiting for transfers between devices, body(): total = lax.psum(projected.astype(jnp.bfloat16), 'grp').astype(jnp.float32)  56.8 us
    dot_general x1, matrix products, body(): jnp.dot(hidden, w_down, preferred_element_type=jnp.float32)  24.7 us
    unnamed x39, local copies, waits for them, and re-layouts  19.9 us
    all_to_all x1, waiting for transfers between devices, body(): lax.all_to_all(mixed, 'req', split_axis=0, concat_axis=0, tiled=True)  16.7 us
    dot_general x1, matrix products, body(): gate = jnp.dot(piece, w_gate, preferred_element_type=jnp.float32)  10.2 us
  transfers between devices with their start and end apart: 7, of which 5 were waited for; matrix products, arithmetic and copies ran while one was open for 15% of the time, Pallas kernels for 0%

commit v1 on v0

--- a/solution.py
+++ b/solution.py
@@ -150,7 +150,9 @@
     )
     residual = own_rows + RESIDUAL_MULT * attn_part
     mlp_in = normalize(residual, mlp_gain).astype(jnp.bfloat16)
-    piece = lax.all_gather(mlp_in, "req", axis=0, tiled=True)
+    piece = jnp.concatenate(
+        lax.all_to_all(jnp.stack([mlp_in] * lax.axis_size("req")), "req", 0, 0), axis=0
+    )
     gate = jnp.dot(piece, w_gate, preferred_element_type=jnp.float32)
     upper = jnp.dot(piece, w_up, preferred_element_type=jnp.float32)
     hidden = (jax.nn.silu(gate) * upper).astype(jnp.bfloat16)

time: 482 us -> 603 us (1.25)
  blocking collectives: 0 us -> 193 us
  waiting for transfers between devices: 267 us -> 191 us
  local copies, waits for them, and re-layouts: 80.5 us -> 88.5 us
    all_to_all x0 -> x1, blocking collectives: none -> 193 us  [body(): lax.all_to_all(jnp.stack([mlp_in] * lax.axis_size('req')), 'req', 0, 0)]
    all_gather x1 -> x0, waiting for transfers between devices: 72.5 us -> none  [body(): piece = lax.all_gather(mlp_in, 'req', axis=0, tiled=True)]
    unnamed x39 -> x47, local copies, waits for them, and re-layouts: 19.9 us -> 25.8 us
  transfers between devices with their start and end apart: 7 -> 6, of which waited for: 5 -> 4; matrix products, arithmetic and copies ran while one was open for 15% -> 12% of each run, Pallas kernels for 0% -> 0%
where the time goes in v1:
time: 603 us; the launch traced here: 596 us
  blocking collectives  193 us (32%)
  waiting for transfers between devices  191 us (32%)
  local copies, waits for them, and re-layouts  88.5 us (15%)
  matrix products  48.1 us (8%)
  other arithmetic  31.7 us (5%)
  starting transfers between devices  28.6 us (5%)
  between operations  14.9 us (2%)
    all_to_all x1, blocking collectives, body(): lax.all_to_all(jnp.stack([mlp_in] * lax.axis_size('req')), 'req', 0, 0)  193 us
    reduce_scatter x1, waiting for transfers between devices, body(): lax.psum_scatter(jnp.dot(hidden, w_down, preferred_element_type=jnp.float...  112 us
    psum x1, waiting for transfers between devices, body(): total = lax.psum(projected.astype(jnp.bfloat16), 'grp').astype(jnp.float32)  56.8 us
    unnamed x47, local copies, waits for them, and re-layouts  25.8 us
    dot_general x1, matrix products, body(): jnp.dot(hidden, w_down, preferred_element_type=jnp.float32)  24.2 us
    all_to_all x1, waiting for transfers between devices, body(): lax.all_to_all(mixed, 'req', split_axis=0, concat_axis=0, tiled=True)  16.7 us
  transfers between devices with their start and end apart: 6, of which 4 were waited for; matrix products, arithmetic and copies ran while one was open for 12% of the time, Pallas kernels for 0%

profile of v1, /device:TPU:0, one launch (start us, length us, event | category | flops | bytes accessed | tf_op | source)
XLA Modules:
  0.0 595.8 jit_solution(4514401828490578951)
XLA Ops:
  26.3 8.4 %all-to-all-start.1 = ((bf16[32,32,128]{2,1,0:T(8,128)(2,1)}), bf16[32,32,128]{2,1,0:T(8,128)(2,1)S(1)}, u32[]{:S(2)}, u32[]{:S(2)}) async-start(bf16[32,32,128]{2,1,0:T(8,128)(2,1)} %bitcast.10), calls=%async_computation.1 | async-start | bytes 524288 | tf_op jit(solution)/shard_map/all_to_all | solution.py:137
  37.3 7.1 %gather_fusion.2 = s32[1024]{0:T(1024)S(1)} fusion(s32[32,16]{1,0:T(8,128)S(1)} %reshape_squeeze.3, s32[1024]{0:T(1024)S(1)} %reshape.579), kind=kCustom, calls=%fused_computation.6 | custom fusion | bytes 16384 | tf_op jit(solution)/shard_map/jit(take_along_axis)/gather | solution.py:69
  48.2 5.1 gather_fusion
  56.6 7.5 %all-to-all-start = ((bf16[32,32,128]{2,1,0:T(8,128)(2,1)}), bf16[32,32,128]{2,1,0:T(8,128)(2,1)}, u32[]{:S(2)}, u32[]{:S(2)}) async-start(bf16[32,32,128]{2,1,0:T(8,128)(2,1)} %bitcast.5), calls=%async_computation | async-start | bytes 524288 | tf_op jit(solution)/shard_map/all_to_all | solution.py:138
  67.4 5.7 all-to-all-done
  73.1 5.1 all-to-all-start.2
  81.8 6.5 %scatter_fusion.1 = bf16[8192,128]{1,0:T(8,128)(2,1)} fusion(bf16[8192,128]{1,0:T(8,128)(2,1)} %bitcast.53, s32[1024]{0:T(1024)S(1)} %broadcast_select_fusion.5, bf16[1024,128]{1,0:T(8,128)(2,1)S(1)} %reshape.593), kind=kCustom, calls=%fused_computation.8 | custom fusion | bytes 790528
  92.2 6.9 %scatter_fusion = bf16[8192,128]{1,0:T(8,128)(2,1)} fusion(bf16[8192,128]{1,0:T(8,128)(2,1)} %bitcast.50, s32[1024]{0:T(1024)S(1)} %broadcast_select_fusion.5, bf16[1024,128]{1,0:T(8,128)(2,1)} %bitcast.6), kind=kCustom, calls=%fused_computation.7 | custom fusion | bytes 790528
  99.2 4.0 gather_fusion.4
  103.2 4.6 broadcast_select_fusion.1
  107.7 8.2 %reshape.515 = bf16[32,256,2,64]{3,2,1,0:T(2,128)(2,1)} reshape(bf16[512,16,128]{2,1,0:T(8,128)(2,1)} %get-tuple-element.22) | data formatting | bytes 4194304 | tf_op jit(solution)/shard_map/reshape | solution.py:77
  116.0 8.3 %reshape.518 = bf16[32,256,2,64]{3,2,1,0:T(2,128)(2,1)} reshape(bf16[512,16,128]{2,1,0:T(8,128)(2,1)} %get-tuple-element.23) | data formatting | bytes 4194304 | tf_op jit(solution)/shard_map/reshape | solution.py:74
  128.1 4.0 fusion.7
  136.0 4.9 fusion.49
  140.9 4.5 convert_bitcast_fusion
  147.9 4.7 reshape.520
  152.6 7.5 %all-to-all-start.3 = ((bf16[32,32,512]{2,1,0:T(8,128)(2,1)}), bf16[32,32,512]{2,1,0:T(8,128)(2,1)S(1)}, u32[]{:S(2)}, u32[]{:S(2)}) async-start(bf16[32,32,512]{2,1,0:T(8,128)(2,1)} %reshape.520), calls=%async_computation.3 | async-start | bytes 2097152 | tf_op jit(solution)/shard_map/all_to_all | solution.py:143
  160.2 16.7 %all-to-all-done.3 = bf16[32,32,512]{2,1,0:T(8,128)(2,1)S(1)} async-done(((bf16[32,32,512]{2,1,0:T(8,128)(2,1)}), bf16[32,32,512]{2,1,0:T(8,128)(2,1)S(1)}, u32[]{:S(2)}, u32[]{:S(2)}) %all-to-all-start.3) | async-done | bytes 1048608 | tf_op jit(solution)/shard_map/all_to_all | solution.py:143
  183.3 56.8 %all-reduce.2.cloned.1.call-done = bf16[512,2048]{1,0:T(8,128)(2,1)} async-done(((bf16[512,2048]{1,0:T(8,128)(2,1)}), bf16[512,2048]{1,0:T(8,128)(2,1)}) %all-reduce.2.cloned.1.call-update) | async-done | bytes 2097168 | tf_op jit(solution)/shard_map/psum | solution.py:146
  245.2 192.5 %all_to_all.25 = bf16[32,128,2048]{2,1,0:T(8,128)(2,1)S(1)} all-to-all(bf16[32,128,2048]{2,1,0:T(8,128)(2,1)S(1)} %stack.2), channel_id=1, replica_groups=mesh['req'=32,'grp'=4] {'req'}, dimensions={0} | all-to-all | bytes 33554432 | tf_op jit(solution)/shard_map/all_to_all | solution.py:154
  437.7 5.7 copy-done.2
  443.5 6.3 %fusion.50 = f32[4096,256]{1,0:T(8,128)} fusion(bf16[4096,2048]{1,0:T(8,128)(2,1)S(1)} %bitcast.56, bf16[2048,256]{1,0:T(8,128)(2,1)S(1)} %copy-done.16), kind=kOutput, calls=%fused_computation.133 | convolution fusion | flops 4294967296 | bytes 22020096 | tf_op jit(solution)/shard_map/dot_general | solution.py:156
  449.8 24.2 %convolution_convert_fusion = bf16[4096,2048]{1,0:T(8,128)(2,1)} fusion(bf16[256,2048]{1,0:T(8,128)(2,1)S(1)} %copy-done.17, bf16[4096,2048]{1,0:T(8,128)(2,1)} %bitcast.57, bf16[2048,256]{1,0:T(8,128)(2,1)S(1)} %copy-done.18, f32[4096,256]{1,0:T(8,128)} %fusion.50), kind=kOutput, calls=%fused_computation.10 | convolution fusion | flops 8604614656 | bytes 39845888 | tf_op jit(solution)/shard_map/dot_general | solution.py:160
  474.1 112.1 %reduce-scatter.2.cloned.1.call-done = bf16[128,2048]{1,0:T(8,128)(2,1)} async-done(((bf16[4096,2048]{1,0:T(8,128)(2,1)}), bf16[128,2048]{1,0:T(8,128)(2,1)}) %reduce-scatter.2.cloned.1.call-update) | async-done | bytes 524304 | tf_op jit(solution)/shard_map/reduce_scatter | solution.py:159
  (115 shorter events, 63.5 us)
Async XLA Ops:
  7.2 172.3 %copy-start = (bf16[512,2048]{1,0:T(8,128)(2,1)S(1)}, bf16[512,2048]{1,0:T(8,128)(2,1)}, u32[]{:S(2)}) copy-start(bf16[512,2048]{1,0:T(8,128)(2,1)} %param.26) | copy-start | bytes 6291460
  7.2 4.8 copy-start.10
  10.6 4.0 copy-start.19
  10.6 4.0 copy-start.20
  12.3 4.7 copy-start.4
  18.8 15.9 %copy-start.9 = (s32[1,512]{1,0:T(1,128)S(1)}, s32[1,512]{1,0:T(1,128)}, u32[]{:S(2)}) copy-start(s32[1,512]{1,0:T(1,128)} %param.35) | copy-start | bytes 6148
  18.8 16.0 %copy-start.12 = (s32[1,32]{1,0:T(1,128)S(1)}, s32[1,32]{1,0:T(1,128)}, u32[]{:S(2)}) copy-start(s32[1,32]{1,0:T(1,128)} %param.34) | copy-start | bytes 388
  18.9 17.9 %copy-start.13 = (s32[1,32]{1,0:T(1,128)S(1)}, s32[1,32]{1,0:T(1,128)}, u32[]{:S(2)}) copy-start(s32[1,32]{1,0:T(1,128)} %param.33) | copy-start | bytes 388
  26.3 30.3 %all-to-all-start.1 = ((bf16[32,32,128]{2,1,0:T(8,128)(2,1)}), bf16[32,32,128]{2,1,0:T(8,128)(2,1)S(1)}, u32[]{:S(2)}, u32[]{:S(2)}) async-start(bf16[32,32,128]{2,1,0:T(8,128)(2,1)} %bitcast.10), calls=%async_computation.1 | async-start | bytes 524288 | tf_op jit(solution)/shard_map/all_to_all | solution.py:137
  37.3 7.2 %copy-start.15 = (s32[2]{0:T(128)S(1)}, s32[2]{0:T(128)}, u32[]{:S(2)}) copy-start(s32[2]{0:T(128)} %constant.139) | copy-start | bytes 28
  37.3 7.3 %copy-start.14 = (s32[2]{0:T(128)S(1)}, s32[2]{0:T(128)}, u32[]{:S(2)}) copy-start(s32[2]{0:T(128)} %constant.136) | copy-start | bytes 28
  56.6 16.4 %all-to-all-start = ((bf16[32,32,128]{2,1,0:T(8,128)(2,1)}), bf16[32,32,128]{2,1,0:T(8,128)(2,1)}, u32[]{:S(2)}, u32[]{:S(2)}) async-start(bf16[32,32,128]{2,1,0:T(8,128)(2,1)} %bitcast.5), calls=%async_computation | async-start | bytes 524288 | tf_op jit(solution)/shard_map/all_to_all | solution.py:138
  73.1 51.2 %all-to-all-start.2 = ((bf16[32,32,512]{2,1,0:T(8,128)(2,1)}), bf16[32,32,512]{2,1,0:T(8,128)(2,1)}, u32[]{:S(2)}, u32[]{:S(2)}) async-start(bf16[32,32,512]{2,1,0:T(8,128)(2,1)} %broadcast_select_fusion.2), calls=%async_computation.2 | async-start | bytes 2097152 | tf_op jit(solution)/shard_map/all_to_all | solution.py:136
  116.0 12.2 %copy-start.5 = (f32[32,32,32]{2,1,0:T(8,128)S(1)}, f32[32,32,32]{2,1,0:T(8,128)}, u32[]{:S(2)}) copy-start(f32[32,32,32]{2,1,0:T(8,128)} %get-tuple-element.16) | copy-start | bytes 393220
  136.0 4.9 copy-start.6
  152.6 24.3 %all-to-all-start.3 = ((bf16[32,32,512]{2,1,0:T(8,128)(2,1)}), bf16[32,32,512]{2,1,0:T(8,128)(2,1)S(1)}, u32[]{:S(2)}, u32[]{:S(2)}) async-start(bf16[32,32,512]{2,1,0:T(8,128)(2,1)} %reshape.520), calls=%async_computation.3 | async-start | bytes 2097152 | tf_op jit(solution)/shard_map/all_to_all | solution.py:143
  160.1 80.1 %all-reduce.2.cloned.1.call-start = ((), (), s32[]{:S(2)}) async-start(), calls=%async_computation.6 | async-start | bytes 4194304 | tf_op jit(solution)/shard_map/psum | solution.py:146
  179.5 62.1 %copy-start.11 = (f32[2048]{0:T(1024)S(1)}, f32[2048]{0:T(1024)}, u32[]{:S(2)}) copy-start(f32[2048]{0:T(1024)} %param.22) | copy-start | bytes 24580
  183.3 402.9 %reduce-scatter.2.cloned.1.call-start = ((), (), s32[]{:S(2)}) async-start(), calls=%async_computation.7 | async-start | bytes 17301504 | tf_op jit(solution)/shard_map/reduce_scatter | solution.py:159
  245.2 198.3 %copy-start.16 = (bf16[2048,256]{1,0:T(8,128)(2,1)S(1)}, bf16[2048,256]{1,0:T(8,128)(2,1)}, u32[]{:S(2)}) copy-start(bf16[2048,256]{1,0:T(8,128)(2,1)} %param.27) | copy-start | bytes 3145732
  437.7 5.7 copy-start.2
  443.5 6.3 %copy-start.17 = (bf16[256,2048]{1,0:T(8,128)(2,1)S(1)}, bf16[256,2048]{1,0:T(8,128)(2,1)}, u32[]{:S(2)}) copy-start(bf16[256,2048]{1,0:T(8,128)(2,1)} %param.29) | copy-start | bytes 3145732
  443.5 6.3 %copy-start.18 = (bf16[2048,256]{1,0:T(8,128)(2,1)S(1)}, bf16[2048,256]{1,0:T(8,128)(2,1)}, u32[]{:S(2)}) copy-start(bf16[2048,256]{1,0:T(8,128)(2,1)} %param.28) | copy-start | bytes 3145732
  474.1 114.5 %copy-start.1 = (bf16[512,2048]{1,0:T(8,128)(2,1)S(1)}, bf16[512,2048]{1,0:T(8,128)(2,1)}, u32[]{:S(2)}) copy-start(bf16[512,2048]{1,0:T(8,128)(2,1)} %param.26) | copy-start | bytes 6291460
  (3 other events, 7.3 us)
Sparse Core Ops, SparseCore 0:
  183.4 56.7 all-reduce.1
  474.2 111.8 reduce-scatter.1
